TPU v7x, 256 devices: a whole 4x4x8 slice. The times are simulated.
256 devices in a mesh: row: 8 (over y, core), col: 32 (over z, x).
Axes of the slice: x: 4, y: 4, z: 8, core: 2. Of those that a mesh axis runs over, the one named last changes fastest.
Arguments:
- solution: float32 [8, 32, 16, 128, 128], P('row', 'col'), may hold values from -6 to 6
- residual: float32 [8, 32, 16, 128, 128], P('row', 'col'), may hold values from -6 to 6, as said below
- prev_direction: float32 [8, 32, 16, 128, 128], P('row', 'col'), may hold values from -6 to 6, as said below
- prev_dot: float32 [128], replicated, may hold values from 262144 to 1048576
- face_lists: int32 [8, 32, 4, 4], P('row', 'col'), may hold values from 0 to 16, as said below
- multiplicity: int32 [8, 32, 16], P('row', 'col'), may hold values from 1 to 2, as said below
- block_pattern: int32 [8, 32, 16, 3], P('row', 'col'), may hold values from 0 to 15, as said below
- schur: float32 [8, 32, 16, 3, 128, 128], P('row', 'col'), may hold values from -1 to 4, as said below
- neumann_inverse: float32 [8, 32, 16, 3, 128, 128], P('row', 'col'), may hold values from 0 to 2, as said below
- coarse_basis: float32 [8, 32, 8, 2048], P('row', 'col'), may hold values from -0.25 to 0.25
- primal_map: int32 [8, 32, 8], P('row', 'col'), may hold values from 0 to 1023, all different within a row
- coarse_inverse: float32 [1024, 1024], P('col'), may hold values from -1 to 1, as said below
Outputs:
- new_solution: float32 [8, 32, 16, 128, 128], P('row', 'col')
- new_residual: float32 [8, 32, 16, 128, 128], P('row', 'col')
- direction: float32 [8, 32, 16, 128, 128], P('row', 'col')
Inputs may be any that keep to these rules, and one draw needn't show every extreme that they name: face_lists[i, j, f, k] names the interface blocks that subdomain (i, j) shares with its neighbour across face f (0 toward row i-1, 1 toward row i+1, 2 toward column j-1, 3 toward column j+1); slot k of a face names the same unknowns as slot k of the neighbour's list for the facing face, and both lists have the same length, 1 to 4 blocks, none on faces at the grid's edge; unused slots hold 16; no block lies on two faces; some face holds 4 blocks. multiplicity is 2 for blocks named in face_lists and 1 for the others. block_pattern[i, j, b, 0] = b; the two other entries of block row b are two other blocks, each of which lists b in turn. `schur`: each subdomain's Schur complement is symmetric positive definite, with positive diagonal and no positive entry off it. `neumann_inverse`: each subdomain's local solve matrix is symmetric positive definite. `coarse_inverse`: symmetric positive definite. `residual`: copies of an unknown held by two subdomains (slot k of facing lists) are equal. `prev_direction`: copies of an unknown held by two subdomains (slot k of facing lists) are equal.
All inputs are finite; a program needn't handle non-finite values.
Results may differ from a plain program's by a relative error of at most 0.0003.
Values sent between devices are 32-bit elements; how exact they have to be, the bound alone decides.
A program may use at most 128 MiB of HBM per device.

v0:
```python
import jax
import jax.numpy as jnp
from jax import lax
from jax.sharding import PartitionSpec as P

HIGH = lax.Precision.HIGHEST


def extended(cells, sides, width):
    for axis, dim in sides:
        count = lax.axis_size(axis)
        ends = count - 1
        head = lax.slice_in_dim(cells, 0, width, axis=dim)
        tail = lax.slice_in_dim(cells, cells.shape[dim] - width, cells.shape[dim], axis=dim)
        cells = jnp.concatenate(
            [
                lax.ppermute(tail, axis, [(i, (i + 1) % count) for i in range(ends)]),
                cells,
                lax.ppermute(head, axis, [((i + 1) % count, i) for i in range(ends)]),
            ],
            axis=dim,
        )
    return cells


def block_product(blocks, pattern, values_in):
    stacked_count, block_count, dofs, cases = values_in.shape
    gathered = jnp.take(values_in, pattern.reshape(-1), axis=1)
    gathered = gathered.reshape(stacked_count, block_count, pattern.shape[1], dofs, cases)
    return jnp.einsum("bkij,vbkjn->vbin", blocks, gathered, precision=HIGH)


def assemble(values_in, faces):
    stacked_count, block_count, dofs, cases = values_in.shape
    flattened = values_in.reshape(stacked_count, block_count, dofs * cases)
    indicator = (faces[..., None] == jnp.arange(block_count)).astype(jnp.float32)
    face_values = jnp.einsum("fkb,vbc->fvkc", indicator, flattened, precision=HIGH)
    row_faces = extended(face_values[0:2], (("row", 0),), 1)
    col_faces = extended(face_values[2:4], (("col", 0),), 1)
    received = jnp.stack([row_faces[0], row_faces[3], col_faces[0], col_faces[3]])
    added = jnp.einsum("fkb,fvkc->vbc", indicator, received, precision=HIGH)
    return (flattened + added).reshape(values_in.shape)


def precondition(residual, weight, faces, pattern, neumann, basis, primal_map, inverse_rows):
    scaled = residual * weight
    local_term = block_product(neumann, pattern, scaled[None])[0]
    cases = residual.shape[-1]
    coarse_local = jnp.dot(basis, scaled.reshape(-1, cases), precision=HIGH)
    owned_count, coarse_total_rows = inverse_rows.shape
    indicator = (primal_map[:, None] == jnp.arange(coarse_total_rows)).astype(jnp.float32)
    owned_rhs = lax.psum_scatter(
        jnp.dot(indicator.T, coarse_local, precision=HIGH), "col", scatter_dimension=0, tiled=True
    )
    owned_rhs = lax.psum(owned_rhs, "row")
    columns = inverse_rows
    owned_solution = jnp.dot(
        columns, lax.all_gather(owned_rhs, "col", axis=0, tiled=True), precision=HIGH
    )
    columns = indicator
    own_coarse = jnp.dot(
        columns, lax.all_gather(owned_solution, "col", axis=0, tiled=True), precision=HIGH
    )
    coarse_back = jnp.dot(basis.T, own_coarse, precision=HIGH).reshape(residual.shape)
    return assemble(((local_term + coarse_back) * weight)[None], faces)[0]


def per_device(
    solution,
    residual,
    prev_direction,
    prev_dot,
    face_lists,
    multiplicity,
    block_pattern,
    schur,
    neumann_inverse,
    coarse_basis,
    primal_map,
    coarse_inverse,
):
    faces = face_lists[0, 0]
    pattern = block_pattern[0, 0]
    weight = (1.0 / multiplicity[0, 0].astype(jnp.float32))[:, None, None]
    current = residual[0, 0]
    previous = prev_direction[0, 0]
    precond = precondition(
        current,
        weight,
        faces,
        pattern,
        neumann_inverse[0, 0],
        coarse_basis[0, 0],
        primal_map[0, 0],
        coarse_inverse,
    )
    local_precond_dot = jnp.sum(current * precond * weight, axis=(0, 1))
    precond_dot = lax.psum(local_precond_dot, ("row", "col"))
    direction_mix = precond_dot / prev_dot
    direction = precond + direction_mix * previous
    image = assemble(block_product(schur[0, 0], pattern, direction[None]), faces)[0]
    curvature = lax.psum(jnp.sum(direction * image * weight, axis=(0, 1)), ("row", "col"))
    step_size = precond_dot / curvature
    new_solution = solution[0, 0] + step_size * direction
    new_residual = current - step_size * image
    return (new_solution[None, None], new_residual[None, None], direction[None, None])


def solution(mesh):
    placed = (
        P("row", "col", None, None, None),
        P("row", "col", None, None, None),
        P("row", "col", None, None, None),
        P(),
        P("row", "col", None, None),
        P("row", "col", None),
        P("row", "col", None, None),
        P("row", "col", None, None, None, None),
        P("row", "col", None, None, None, None),
        P("row", "col", None, None),
        P("row", "col", None),
        P("col", None),
    )
    return jax.shard_map(
        per_device,
        mesh=mesh,
        in_specs=placed,
        out_specs=(
            P("row", "col", None, None, None),
            P("row", "col", None, None, None),
            P("row", "col", None, None, None),
        ),
        check_vma=False,
    )
```

profile of v0, /device:TPU:1, one launch (start us, length us, event | category | flops | bytes accessed | tf_op | source)
XLA Modules:
  0.0 597.9 jit_solution(11276702184320067996)
XLA Ops:
  7.2 0.0 copy-start
  7.2 0.0 reduce-scatter.2.cloned.1.call-start
  7.2 0.8 divide_bitcast_fusion
  8.0 1.5 broadcast_multiply_fusion
  9.5 1.5 fusion.35
  11.0 1.5 fusion.38
  12.5 0.0 reduce-scatter.2.cloned.1.call-update
  12.5 2.3 fusion.31
  14.9 0.1 copy.39
  14.9 0.1 reshape_squeeze.4
  15.1 3.6 gather_fusion
  18.7 2.2 bitcast_select_fusion.1
  20.9 0.0 copy-start.9
  20.9 6.2 %fusion.6 = f32[1,16,128,128]{2,3,1,0:T(8,128)} fusion(f32[16,3,128,128]{3,2,1,0:T(8,128)S(1)} %bitcast.147, f32[1,1,16,3,128,128]{5,4,3,2,1,0:T(8,128)S(1)} %copy-done), kind=kOutput, calls=%fused_computation.15 | convolution fusion | flops 1207959552 | bytes 7340032 | tf_op jit(solution)/shard_map/bkij,vbkjn->vbin/dot_general | solution.py:30
  27.1 2.6 copy.44
  29.7 194.6 %reduce-scatter.2.cloned.1.call-done = f32[32,128]{1,0:T(8,128)} async-done(((f32[1024,128]{1,0:T(8,128)}), f32[32,128]{1,0:T(8,128)}) %reduce-scatter.2.cloned.1.call-update) | async-done | bytes 16400 | tf_op jit(solution)/shard_map/reduce_scatter | solution.py:52
  224.3 26.4 %psum.21 = f32[32,128]{1,0:T(8,128)S(1)} all-reduce(f32[32,128]{1,0:T(8,128)} %reduce-scatter.2.cloned.1.call-done), channel_id=1, replica_groups=mesh['row'=8,'col'=32] {'row'}, use_global_device_ids=true, to_apply=%region_1.3 | all-reduce | flops 4096 | bytes 32768 | tf_op jit(solution)/shard_map/psum | solution.py:55
  250.7 35.9 %all_gather.6 = f32[1024,128]{1,0:T(8,128)S(1)} all-gather(f32[32,128]{1,0:T(8,128)S(1)} %psum.21), channel_id=1, replica_groups=mesh['row'=8,'col'=32] {'col'}, dimensions={0}, use_global_device_ids=true | all-gather | bytes 540672 | tf_op jit(solution)/shard_map/all_gather | solution.py:58
  286.5 0.4 convolution_bitcast_fusion.5
  286.9 0.0 copy-start.10
  287.0 35.8 %all_gather.7 = f32[1024,128]{1,0:T(8,128)S(1)} all-gather(f32[32,128]{1,0:T(8,128)S(1)} %convolution_bitcast_fusion.5), channel_id=1, replica_groups=mesh['row'=8,'col'=32] {'col'}, dimensions={0}, use_global_device_ids=true | all-gather | bytes 540672 | tf_op jit(solution)/shard_map/all_gather | solution.py:62
  322.7 0.3 fusion.37
  323.0 2.0 convolution_bitcast_fusion.4
  325.0 2.5 copy.42
  327.6 2.4 reshape.184
  329.9 3.0 convolution_bitcast_fusion.3
  333.0 0.9 fusion.48
  333.9 27.6 %collective-permute-start = (f32[1,1,4,16384]{3,2,0,1:T(4,128)}, f32[1,1,4,16384]{3,2,0,1:T(4,128)}, u32[]{:S(2)}, u32[]{:S(2)}) collective-permute-start(f32[1,1,4,16384]{3,2,0,1:T(4,128)} %get-tuple-element.10), channel_id=1, source_target_pairs={{0,32},{32,64},{64,96},{96,128},{128,160},{160,192},{192,224},{1,3... | collective-permute-start | bytes 786440 | tf_op jit(solution)/shard_map/ppermute | solution.py:17
  361.5 3.8 collective-permute-start.1
  365.4 3.1 collective-permute-start.2
  368.4 1.3 collective-permute-start.3
  369.7 2.5 copy.41
  372.2 2.4 squeeze.32
  374.6 2.4 reshape.183
  377.0 1.6 collective-permute-done.3
  378.6 3.4 fusion.1
  382.0 0.0 copy-start.4
  382.0 0.0 copy-start.13
  382.0 0.9 copy-done.4
  383.0 0.2 copy.54
  383.2 1.0 copy-done.2
  384.1 0.4 fusion.14
  384.5 78.4 %psum.22 = f32[128]{0:T(128)S(1)} all-reduce(f32[128]{0:T(128)S(1)} %fusion.14), channel_id=1, replica_groups=mesh['row'=8,'col'=32] {'row','col'}, use_global_device_ids=true, to_apply=%region_3.5 | all-reduce | flops 128 | bytes 1024 | tf_op jit(solution)/shard_map/psum | solution.py:98
  462.9 2.7 fusion.12
  465.5 3.6 gather_fusion.1
  469.1 2.3 bitcast_select_fusion
  471.5 0.5 copy-done.7
  472.0 6.3 %fusion.9 = f32[1,16,128,128]{2,3,1,0:T(8,128)} fusion(f32[16,3,128,128]{3,2,1,0:T(8,128)S(1)} %bitcast.146, f32[1,1,16,3,128,128]{5,4,3,2,1,0:T(8,128)S(1)} %copy-done.7), kind=kOutput, calls=%fused_computation.16 | convolution fusion | flops 1207959552 | bytes 7340032 | tf_op jit(solution)/shard_map/bkij,vbkjn->vbin/dot_general | solution.py:30
  478.3 2.5 copy.47
  480.8 2.4 reshape.224
  483.2 2.4 reshape.187
  485.6 2.4 convolution_bitcast_fusion.1
  488.0 0.1 fusion.47
  488.1 3.7 collective-permute-start.4
  491.8 1.9 collective-permute-start.5
  493.7 1.9 collective-permute-start.6
  495.7 1.3 collective-permute-start.7
  497.0 2.5 collective-permute-done.5
  499.5 2.2 collective-permute-done.6
  501.7 4.1 collective-permute-done.7
  505.8 1.2 multiply_reduce_fusion
  507.0 1.2 copy.57
  508.2 78.4 %psum.23 = f32[128]{0:T(128)S(1)} all-reduce(f32[128]{0:T(128)S(1)} %bitcast_reduce_fusion), channel_id=1, replica_groups=mesh['row'=8,'col'=32] {'row','col'}, use_global_device_ids=true, to_apply=%region_6.8 | all-reduce | flops 128 | bytes 1024 | tf_op jit(solution)/shard_map/psum | solution.py:102
  586.6 4.5 multiply_add_fusion
  (31 shorter events, 0.1 us)
Async XLA Ops:
  7.2 13.7 %copy-start = (f32[1,1,16,3,128,128]{5,4,3,2,1,0:T(8,128)S(1)}, f32[1,1,16,3,128,128]{5,4,3,2,1,0:T(8,128)}, u32[]{:S(2)}) copy-start(f32[1,1,16,3,128,128]{5,4,3,2,1,0:T(8,128)} %param.22) | copy-start | bytes 9437188
  7.2 3.8 copy-start.11
  7.2 217.1 %reduce-scatter.2.cloned.1.call-start = ((), (), s32[]{:S(2)}) async-start(), calls=%async_computation.1 | async-start | bytes 540672 | tf_op jit(solution)/shard_map/reduce_scatter | solution.py:52
  8.0 6.8 %copy-start.12 = (s32[1,1,16,3]{2,1,3,0:T(1,128)S(1)}, s32[1,1,16,3]{2,1,3,0:T(1,128)}, u32[]{:S(2)}) copy-start(s32[1,1,16,3]{2,1,3,0:T(1,128)} %param.20) | copy-start | bytes 580
  20.9 265.7 %copy-start.9 = (f32[32,1024]{1,0:T(8,128)S(1)}, f32[32,1024]{1,0:T(8,128)}, u32[]{:S(2)}) copy-start(f32[32,1024]{1,0:T(8,128)} %param.25) | copy-start | bytes 393220
  27.1 295.9 %copy-start.8 = (f32[1,1,8,2048]{3,2,1,0:T(8,128)S(1)}, f32[1,1,8,2048]{3,2,1,0:T(8,128)}, u32[]{:S(2)}) copy-start(f32[1,1,8,2048]{3,2,1,0:T(8,128)} %param.23) | copy-start | bytes 196612
  286.9 43.0 %copy-start.10 = (s32[1,1,4,4]{3,2,1,0:T(4,128)S(1)}, s32[1,1,4,4]{3,2,1,0:T(4,128)}, u32[]{:S(2)}) copy-start(s32[1,1,4,4]{3,2,1,0:T(4,128)} %param.18) | copy-start | bytes 196
  333.9 43.1 %collective-permute-start = (f32[1,1,4,16384]{3,2,0,1:T(4,128)}, f32[1,1,4,16384]{3,2,0,1:T(4,128)}, u32[]{:S(2)}, u32[]{:S(2)}) collective-permute-start(f32[1,1,4,16384]{3,2,0,1:T(4,128)} %get-tuple-element.10), channel_id=1, source_target_pairs={{0,32},{32,64},{64,96},{96,128},{128,160},{160,192},{192,224},{1,3... | collective-permute-start | bytes 786440 | tf_op jit(solution)/shard_map/ppermute | solution.py:17
  361.5 15.5 %collective-permute-start.1 = (f32[1,1,4,16384]{3,2,0,1:T(4,128)}, f32[1,1,4,16384]{3,2,0,1:T(4,128)}, u32[]{:S(2)}, u32[]{:S(2)}) collective-permute-start(f32[1,1,4,16384]{3,2,0,1:T(4,128)} %get-tuple-element.13), channel_id=1, source_target_pairs={{32,0},{64,32},{96,64},{128,96},{160,128},{192,160},{224,192},{33,... | collective-permute-start | bytes 786440 | tf_op jit(solution)/shard_map/ppermute | solution.py:19
  365.4 11.7 %collective-permute-start.2 = (f32[1,1,4,16384]{3,2,0,1:T(4,128)}, f32[1,1,4,16384]{3,2,0,1:T(4,128)}, u32[]{:S(2)}, u32[]{:S(2)}) collective-permute-start(f32[1,1,4,16384]{3,2,0,1:T(4,128)} %get-tuple-element.12), channel_id=1, source_target_pairs={{0,1},{1,2},{2,3},{3,4},{4,5},{5,6},{6,7},{7,8},{8,9},{9,10},{10,1... | collective-permute-start | bytes 786440 | tf_op jit(solution)/shard_map/ppermute | solution.py:17
  368.4 10.2 %collective-permute-start.3 = (f32[1,1,4,16384]{3,2,0,1:T(4,128)S(1)}, f32[1,1,4,16384]{3,2,0,1:T(4,128)}, u32[]{:S(2)}, u32[]{:S(2)}) collective-permute-start(f32[1,1,4,16384]{3,2,0,1:T(4,128)S(1)} %get-tuple-element.11), channel_id=1, source_target_pairs={{1,0},{2,1},{3,2},{4,3},{5,4},{6,5},{7,6},{8,7},{9,8},{10,9},{11,1... | collective-permute-start | bytes 786440 | tf_op jit(solution)/shard_map/ppermute | solution.py:19
  378.6 5.5 copy-start.1
  382.0 1.0 copy-start.4
  382.0 80.9 %copy-start.13 = (f32[128]{0:T(128)S(1)}, f32[128]{0:T(128)}, u32[]{:S(2)}) copy-start(f32[128]{0:T(128)} %param.17) | copy-start | bytes 1540
  383.2 1.0 copy-start.2
  469.1 2.8 copy-start.7
  485.6 20.1 %copy-start.3 = (f32[1,16,16384]{2,1,0:T(8,128)S(1)}, f32[1,16,16384]{2,1,0:T(8,128)}, u32[]{:S(2)}) copy-start(f32[1,16,16384]{2,1,0:T(8,128)} %squeeze.32) | copy-start | bytes 3145732
  485.6 20.1 %copy-start.5 = (f32[1,16,16384]{2,1,0:T(8,128)S(1)}, f32[1,16,16384]{2,1,0:T(8,128)}, u32[]{:S(2)}) copy-start(f32[1,16,16384]{2,1,0:T(8,128)} %copy-done.4) | copy-start | bytes 3145732
  485.6 20.1 %copy-start.6 = (f32[1,16,16384]{2,1,0:T(8,128)S(1)}, f32[1,16,16384]{2,1,0:T(8,128)}, u32[]{:S(2)}) copy-start(f32[1,16,16384]{2,1,0:T(8,128)} %reshape.187) | copy-start | bytes 3145732
  488.1 8.9 %collective-permute-start.4 = (f32[1,1,4,16384]{3,2,0,1:T(4,128)S(1)}, f32[1,1,4,16384]{3,2,0,1:T(4,128)S(1)}, u32[]{:S(2)}, u32[]{:S(2)}) collective-permute-start(f32[1,1,4,16384]{3,2,0,1:T(4,128)S(1)} %get-tuple-element.6), channel_id=1, source_target_pairs={{0,32},{32,64},{64,96},{96,128},{128,160},{160,192},{192,224},{1,3... | collective-permute-start | bytes 786440 | tf_op jit(solution)/shard_map/ppermute | solution.py:17
  491.8 7.7 %collective-permute-start.5 = (f32[1,1,4,16384]{3,2,0,1:T(4,128)S(1)}, f32[1,1,4,16384]{3,2,0,1:T(4,128)S(1)}, u32[]{:S(2)}, u32[]{:S(2)}) collective-permute-start(f32[1,1,4,16384]{3,2,0,1:T(4,128)S(1)} %get-tuple-element.9), channel_id=1, source_target_pairs={{32,0},{64,32},{96,64},{128,96},{160,128},{192,160},{224,192},{33,... | collective-permute-start | bytes 786440 | tf_op jit(solution)/shard_map/ppermute | solution.py:19
  493.7 7.9 %collective-permute-start.6 = (f32[1,1,4,16384]{3,2,0,1:T(4,128)S(1)}, f32[1,1,4,16384]{3,2,0,1:T(4,128)S(1)}, u32[]{:S(2)}, u32[]{:S(2)}) collective-permute-start(f32[1,1,4,16384]{3,2,0,1:T(4,128)S(1)} %get-tuple-element.8), channel_id=1, source_target_pairs={{0,1},{1,2},{2,3},{3,4},{4,5},{5,6},{6,7},{7,8},{8,9},{9,10},{10,1... | collective-permute-start | bytes 786440 | tf_op jit(solution)/shard_map/ppermute | solution.py:17
  495.7 10.1 %collective-permute-start.7 = (f32[1,1,4,16384]{3,2,0,1:T(4,128)S(1)}, f32[1,1,4,16384]{3,2,0,1:T(4,128)S(1)}, u32[]{:S(2)}, u32[]{:S(2)}) collective-permute-start(f32[1,1,4,16384]{3,2,0,1:T(4,128)S(1)} %get-tuple-element.7), channel_id=1, source_target_pairs={{1,0},{2,1},{3,2},{4,3},{5,4},{6,5},{7,6},{8,7},{9,8},{10,9},{11,1... | collective-permute-start | bytes 786440 | tf_op jit(solution)/shard_map/ppermute | solution.py:19
Sparse Core Ops, SparseCore 0:
  12.7 211.5 reduce-scatter.1
where the time goes:
time: 599 us; the launch traced here: 598 us
  blocking collectives  255 us (43%)
  waiting for transfers between devices  205 us (34%)
  starting transfers between devices  44.6 us (7%)
  local copies, waits for them, and re-layouts  34.4 us (6%)
  matrix products  28.1 us (5%)
  other arithmetic  16.6 us (3%)
  between operations  14.3 us (2%)
    reduce_scatter x1, waiting for transfers between devices, precondition(): lax.psum_scatter(jnp.dot(indicator.T, coarse_local, precision=HIGH), 'col...  195 us
    psum x1, blocking collectives, per_device(): lax.psum(jnp.sum(direction * image * weight, axis=(0, 1)), ('row', 'col'))  78.4 us
    psum x1, blocking collectives, per_device(): precond_dot = lax.psum(local_precond_dot, ('row', 'col'))  78.4 us
    ppermute x4, starting transfers between devices, extended(): lax.ppermute(tail, axis, [(i, (i + 1) % count) for i in range(ends)])  36.3 us
    all_gather x1, blocking collectives, precondition(): lax.all_gather(owned_rhs, 'col', axis=0, tiled=True)  35.9 us
    all_gather x1, blocking collectives, precondition(): lax.all_gather(owned_solution, 'col', axis=0, tiled=True)  35.8 us
    psum x1, blocking collectives, precondition(): owned_rhs = lax.psum(owned_rhs, 'row')  26.4 us
    dot_general x2, matrix products, block_product(): return jnp.einsum('bkij,vbkjn->vbin', blocks, gathered, precision=HIGH)  12.5 us
  transfers between devices with their start and end apart: 9, of which 5 were waited for; matrix products, arithmetic and copies ran while one was open for 4% of the time, Pallas kernels for 0%

commit v1 on v0

--- a/solution.py
+++ b/solution.py
@@ -4,6 +4,11 @@
 from jax.sharding import PartitionSpec as P
 
 HIGH = lax.Precision.HIGHEST
+
+
+def tiled_gather(x, axis, dim):
+    copies = jnp.concatenate([x] * lax.axis_size(axis), axis=dim)
+    return lax.all_to_all(copies, axis, dim, dim, tiled=True)
 
 
 def extended(cells, sides, width):
@@ -54,9 +59,7 @@
     )
     owned_rhs = lax.psum(owned_rhs, "row")
     columns = inverse_rows
-    owned_solution = jnp.dot(
-        columns, lax.all_gather(owned_rhs, "col", axis=0, tiled=True), precision=HIGH
-    )
+    owned_solution = jnp.dot(columns, tiled_gather(owned_rhs, "col", 0), precision=HIGH)
     columns = indicator
     own_coarse = jnp.dot(
         columns, lax.all_gather(owned_solution, "col", axis=0, tiled=True), precision=HIGH

time: 599 us -> 574 us (0.958)
  blocking collectives: 255 us -> 220 us
  waiting for transfers between devices: 205 us -> 218 us
    all_gather x1 -> x0, blocking collectives: 35.9 us -> none  [precondition(): lax.all_gather(owned_rhs, 'col', axis=0, tiled=True)]
    reduce_scatter x1, waiting for transfers between devices: 195 us -> 206 us  [precondition(): lax.psum_scatter(jnp.dot(indicator.T, coarse_local, precision=HIGH), 'col...]
    ppermute x4, starting transfers between devices: 36.3 us -> 26.6 us  [extended(): lax.ppermute(tail, axis, [(i, (i + 1) % count) for i in range(ends)])]
    all_to_all x0 -> x1, starting transfers between devices: none -> 6.74 us  [tiled_gather(): return lax.all_to_all(copies, axis, dim, dim, tiled=True)]
  transfers between devices with their start and end apart: 9 -> 10, of which waited for: 5 -> 6; matrix products, arithmetic and copies ran while one was open for 4% -> 4% of each run, Pallas kernels for 0% -> 0%
where the time goes in v1:
time: 574 us; the launch traced here: 573 us
  blocking collectives  220 us (38%)
  waiting for transfers between devices  218 us (38%)
  starting transfers between devices  40 us (7%)
  local copies, waits for them, and re-layouts  35.3 us (6%)
  matrix products  29.2 us (5%)
  other arithmetic  16.7 us (3%)
  between operations  14.6 us (3%)
    reduce_scatter x1, waiting for transfers between devices, precondition(): lax.psum_scatter(jnp.dot(indicator.T, coarse_local, precision=HIGH), 'col...  206 us
    psum x1, blocking collectives, per_device(): lax.psum(jnp.sum(direction * image * weight, axis=(0, 1)), ('row', 'col'))  78.4 us
    psum x1, blocking collectives, per_device(): precond_dot = lax.psum(local_precond_dot, ('row', 'col'))  77.9 us
    all_gather x1, blocking collectives, precondition(): lax.all_gather(owned_solution, 'col', axis=0, tiled=True)  37 us
    ppermute x4, starting transfers between devices, extended(): lax.ppermute(tail, axis, [(i, (i + 1) % count) for i in range(ends)])  26.6 us
    psum x1, blocking collectives, precondition(): owned_rhs = lax.psum(owned_rhs, 'row')  26.4 us
    dot_general x2, matrix products, block_product(): return jnp.einsum('bkij,vbkjn->vbin', blocks, gathered, precision=HIGH)  12.5 us
  transfers between devices with their start and end apart: 10, of which 6 were waited for; matrix products, arithmetic and copies ran while one was open for 4% of the time, Pallas kernels for 0%

profile of v1, /device:TPU:1, one launch (start us, length us, event | category | flops | bytes accessed | tf_op | source)
XLA Modules:
  0.0 573.2 jit_solution(7345887871936899259)
XLA Ops:
  7.2 0.0 copy-start
  7.2 0.0 reduce-scatter.2.cloned.1.call-start
  7.2 0.8 divide_bitcast_fusion
  8.1 1.5 broadcast_multiply_fusion
  9.5 1.5 fusion.35
  11.0 1.5 fusion.38
  12.5 0.0 reduce-scatter.2.cloned.1.call-update
  12.5 0.1 copy.39
  12.6 0.1 reshape_squeeze.4
  12.7 2.3 fusion.31
  15.1 3.6 gather_fusion
  18.7 205.6 %reduce-scatter.2.cloned.1.call-done = f32[32,128]{1,0:T(8,128)} async-done(((f32[1024,128]{1,0:T(8,128)}), f32[32,128]{1,0:T(8,128)}) %reduce-scatter.2.cloned.1.call-update) | async-done | bytes 16400 | tf_op jit(solution)/shard_map/reduce_scatter | solution.py:57
  224.3 26.4 %psum.21 = f32[32,128]{1,0:T(8,128)S(1)} all-reduce(f32[32,128]{1,0:T(8,128)} %reduce-scatter.2.cloned.1.call-done), channel_id=1, replica_groups=mesh['row'=8,'col'=32] {'row'}, use_global_device_ids=true, to_apply=%region_1.3 | all-reduce | flops 4096 | bytes 32768 | tf_op jit(solution)/shard_map/psum | solution.py:60
  251.0 0.0 copy-start.8
  251.0 0.8 copy-done.8
  251.8 6.7 %all-to-all-start = ((f32[32,32,128]{2,1,0:T(8,128)}), f32[32,32,128]{2,1,0:T(8,128)}, u32[]{:S(2)}, u32[]{:S(2)}) async-start(f32[32,32,128]{2,1,0:T(8,128)} %bitcast.156), calls=%async_computation.1 | async-start | bytes 1048576 | tf_op jit(solution)/shard_map/all_to_all | solution.py:11
  258.6 2.2 bitcast_select_fusion.1
  260.7 0.0 copy-start.10
  260.7 6.2 %fusion.6 = f32[1,16,128,128]{2,3,1,0:T(8,128)} fusion(f32[16,3,128,128]{3,2,1,0:T(8,128)S(1)} %bitcast.149, f32[1,1,16,3,128,128]{5,4,3,2,1,0:T(8,128)S(1)} %copy-done), kind=kOutput, calls=%fused_computation.15 | convolution fusion | flops 1207959552 | bytes 7340032 | tf_op jit(solution)/shard_map/bkij,vbkjn->vbin/dot_general | solution.py:35
  267.0 2.6 copy.44
  269.5 1.9 all-to-all-done
  271.4 1.4 convolution_bitcast_fusion.5
  272.9 37.0 %all_gather.3 = f32[1024,128]{1,0:T(8,128)S(1)} all-gather(f32[32,128]{1,0:T(8,128)S(1)} %convolution_bitcast_fusion.5), channel_id=1, replica_groups=mesh['row'=8,'col'=32] {'col'}, dimensions={0}, use_global_device_ids=true | all-gather | bytes 540672 | tf_op jit(solution)/shard_map/all_gather | solution.py:65
  309.9 0.3 fusion.37
  310.2 2.0 convolution_bitcast_fusion.4
  312.2 2.5 copy.42
  314.7 2.4 reshape.186
  317.1 3.0 convolution_bitcast_fusion.3
  320.2 0.9 fusion.48
  321.1 18.9 %collective-permute-start = (f32[1,1,4,16384]{3,2,0,1:T(4,128)}, f32[1,1,4,16384]{3,2,0,1:T(4,128)}, u32[]{:S(2)}, u32[]{:S(2)}) collective-permute-start(f32[1,1,4,16384]{3,2,0,1:T(4,128)} %get-tuple-element.10), channel_id=1, source_target_pairs={{0,32},{32,64},{64,96},{96,128},{128,160},{160,192},{192,224},{1,3... | collective-permute-start | bytes 786440 | tf_op jit(solution)/shard_map/ppermute | solution.py:22
  340.0 2.1 collective-permute-start.1
  342.2 2.6 collective-permute-start.2
  344.7 1.3 collective-permute-start.3
  346.0 2.5 copy.41
  348.6 2.4 squeeze.32
  350.9 2.4 reshape.185
  353.3 1.6 collective-permute-done.3
  354.9 3.4 fusion.1
  358.3 0.9 copy-done.4
  359.3 0.2 copy.54
  359.5 1.0 copy-done.2
  360.4 0.4 fusion.14
  360.8 77.9 %psum.22 = f32[128]{0:T(128)S(1)} all-reduce(f32[128]{0:T(128)S(1)} %fusion.14), channel_id=1, replica_groups=mesh['row'=8,'col'=32] {'row','col'}, use_global_device_ids=true, to_apply=%region_3.5 | all-reduce | flops 128 | bytes 1024 | tf_op jit(solution)/shard_map/psum | solution.py:101
  438.8 2.7 fusion.12
  441.4 3.6 gather_fusion.1
  445.0 2.3 bitcast_select_fusion
  447.4 0.5 copy-done.7
  447.9 6.3 %fusion.9 = f32[1,16,128,128]{2,3,1,0:T(8,128)} fusion(f32[16,3,128,128]{3,2,1,0:T(8,128)S(1)} %bitcast.148, f32[1,1,16,3,128,128]{5,4,3,2,1,0:T(8,128)S(1)} %copy-done.7), kind=kOutput, calls=%fused_computation.16 | convolution fusion | flops 1207959552 | bytes 7340032 | tf_op jit(solution)/shard_map/bkij,vbkjn->vbin/dot_general | solution.py:35
  454.1 2.5 copy.47
  456.7 2.4 reshape.226
  459.1 2.4 reshape.189
  461.5 2.4 convolution_bitcast_fusion.1
  463.9 0.1 fusion.47
  464.0 3.1 collective-permute-start.4
  467.1 1.9 collective-permute-start.5
  469.0 1.9 collective-permute-start.6
  471.0 1.3 collective-permute-start.7
  472.3 2.5 collective-permute-done.5
  474.8 2.2 collective-permute-done.6
  477.0 4.1 collective-permute-done.7
  481.1 1.2 multiply_reduce_fusion
  482.3 1.2 copy.57
  483.5 78.4 %psum.23 = f32[128]{0:T(128)S(1)} all-reduce(f32[128]{0:T(128)S(1)} %bitcast_reduce_fusion), channel_id=1, replica_groups=mesh['row'=8,'col'=32] {'row','col'}, use_global_device_ids=true, to_apply=%region_6.8 | all-reduce | flops 128 | bytes 1024 | tf_op jit(solution)/shard_map/psum | solution.py:105
  561.9 4.5 multiply_add_fusion
  (66 shorter events, 0.2 us)
Async XLA Ops:
  7.2 253.6 %copy-start = (f32[1,1,16,3,128,128]{5,4,3,2,1,0:T(8,128)S(1)}, f32[1,1,16,3,128,128]{5,4,3,2,1,0:T(8,128)}, u32[]{:S(2)}) copy-start(f32[1,1,16,3,128,128]{5,4,3,2,1,0:T(8,128)} %param.22) | copy-start | bytes 9437188
  7.2 3.8 copy-start.12
  7.2 5.3 copy-start.13
  7.2 217.1 %reduce-scatter.2.cloned.1.call-start = ((), (), s32[]{:S(2)}) async-start(), calls=%async_computation.2 | async-start | bytes 540672 | tf_op jit(solution)/shard_map/reduce_scatter | solution.py:57
  251.0 0.8 copy-start.8
  251.8 19.6 %all-to-all-start = ((f32[32,32,128]{2,1,0:T(8,128)}), f32[32,32,128]{2,1,0:T(8,128)}, u32[]{:S(2)}, u32[]{:S(2)}) async-start(f32[32,32,128]{2,1,0:T(8,128)} %bitcast.156), calls=%async_computation.1 | async-start | bytes 1048576 | tf_op jit(solution)/shard_map/all_to_all | solution.py:11
  260.7 10.7 %copy-start.10 = (f32[32,1024]{1,0:T(8,128)S(1)}, f32[32,1024]{1,0:T(8,128)}, u32[]{:S(2)}) copy-start(f32[32,1024]{1,0:T(8,128)} %param.25) | copy-start | bytes 393220
  267.0 43.2 %copy-start.9 = (f32[1,1,8,2048]{3,2,1,0:T(8,128)S(1)}, f32[1,1,8,2048]{3,2,1,0:T(8,128)}, u32[]{:S(2)}) copy-start(f32[1,1,8,2048]{3,2,1,0:T(8,128)} %param.23) | copy-start | bytes 196612
  272.9 44.2 %copy-start.11 = (s32[1,1,4,4]{3,2,1,0:T(4,128)S(1)}, s32[1,1,4,4]{3,2,1,0:T(4,128)}, u32[]{:S(2)}) copy-start(s32[1,1,4,4]{3,2,1,0:T(4,128)} %param.18) | copy-start | bytes 196
  321.1 32.2 %collective-permute-start = (f32[1,1,4,16384]{3,2,0,1:T(4,128)}, f32[1,1,4,16384]{3,2,0,1:T(4,128)}, u32[]{:S(2)}, u32[]{:S(2)}) collective-permute-start(f32[1,1,4,16384]{3,2,0,1:T(4,128)} %get-tuple-element.10), channel_id=1, source_target_pairs={{0,32},{32,64},{64,96},{96,128},{128,160},{160,192},{192,224},{1,3... | collective-permute-start | bytes 786440 | tf_op jit(solution)/shard_map/ppermute | solution.py:22
  340.0 13.3 %collective-permute-start.1 = (f32[1,1,4,16384]{3,2,0,1:T(4,128)}, f32[1,1,4,16384]{3,2,0,1:T(4,128)}, u32[]{:S(2)}, u32[]{:S(2)}) collective-permute-start(f32[1,1,4,16384]{3,2,0,1:T(4,128)} %get-tuple-element.13), channel_id=1, source_target_pairs={{32,0},{64,32},{96,64},{128,96},{160,128},{192,160},{224,192},{33,... | collective-permute-start | bytes 786440 | tf_op jit(solution)/shard_map/ppermute | solution.py:24
  342.2 11.2 %collective-permute-start.2 = (f32[1,1,4,16384]{3,2,0,1:T(4,128)}, f32[1,1,4,16384]{3,2,0,1:T(4,128)}, u32[]{:S(2)}, u32[]{:S(2)}) collective-permute-start(f32[1,1,4,16384]{3,2,0,1:T(4,128)} %get-tuple-element.12), channel_id=1, source_target_pairs={{0,1},{1,2},{2,3},{3,4},{4,5},{5,6},{6,7},{7,8},{8,9},{9,10},{10,1... | collective-permute-start | bytes 786440 | tf_op jit(solution)/shard_map/ppermute | solution.py:22
  344.7 10.2 %collective-permute-start.3 = (f32[1,1,4,16384]{3,2,0,1:T(4,128)S(1)}, f32[1,1,4,16384]{3,2,0,1:T(4,128)}, u32[]{:S(2)}, u32[]{:S(2)}) collective-permute-start(f32[1,1,4,16384]{3,2,0,1:T(4,128)S(1)} %get-tuple-element.11), channel_id=1, source_target_pairs={{1,0},{2,1},{3,2},{4,3},{5,4},{6,5},{7,6},{8,7},{9,8},{10,9},{11,1... | collective-permute-start | bytes 786440 | tf_op jit(solution)/shard_map/ppermute | solution.py:24
  354.9 5.5 copy-start.1
  358.3 1.0 copy-start.4
  358.3 80.4 %copy-start.14 = (f32[128]{0:T(128)S(1)}, f32[128]{0:T(128)}, u32[]{:S(2)}) copy-start(f32[128]{0:T(128)} %param.17) | copy-start | bytes 1540
  359.5 1.0 copy-start.2
  445.0 2.8 copy-start.7
  461.5 19.6 %copy-start.3 = (f32[1,16,16384]{2,1,0:T(8,128)S(1)}, f32[1,16,16384]{2,1,0:T(8,128)}, u32[]{:S(2)}) copy-start(f32[1,16,16384]{2,1,0:T(8,128)} %squeeze.32) | copy-start | bytes 3145732
  461.5 19.6 %copy-start.5 = (f32[1,16,16384]{2,1,0:T(8,128)S(1)}, f32[1,16,16384]{2,1,0:T(8,128)}, u32[]{:S(2)}) copy-start(f32[1,16,16384]{2,1,0:T(8,128)} %copy-done.4) | copy-start | bytes 3145732
  461.5 19.6 %copy-start.6 = (f32[1,16,16384]{2,1,0:T(8,128)S(1)}, f32[1,16,16384]{2,1,0:T(8,128)}, u32[]{:S(2)}) copy-start(f32[1,16,16384]{2,1,0:T(8,128)} %reshape.189) | copy-start | bytes 3145732
  464.0 8.3 %collective-permute-start.4 = (f32[1,1,4,16384]{3,2,0,1:T(4,128)S(1)}, f32[1,1,4,16384]{3,2,0,1:T(4,128)S(1)}, u32[]{:S(2)}, u32[]{:S(2)}) collective-permute-start(f32[1,1,4,16384]{3,2,0,1:T(4,128)S(1)} %get-tuple-element.6), channel_id=1, source_target_pairs={{0,32},{32,64},{64,96},{96,128},{128,160},{160,192},{192,224},{1,3... | collective-permute-start | bytes 786440 | tf_op jit(solution)/shard_map/ppermute | solution.py:22
  467.1 7.7 %collective-permute-start.5 = (f32[1,1,4,16384]{3,2,0,1:T(4,128)S(1)}, f32[1,1,4,16384]{3,2,0,1:T(4,128)S(1)}, u32[]{:S(2)}, u32[]{:S(2)}) collective-permute-start(f32[1,1,4,16384]{3,2,0,1:T(4,128)S(1)} %get-tuple-element.9), channel_id=1, source_target_pairs={{32,0},{64,32},{96,64},{128,96},{160,128},{192,160},{224,192},{33,... | collective-permute-start | bytes 786440 | tf_op jit(solution)/shard_map/ppermute | solution.py:24
  469.0 7.9 %collective-permute-start.6 = (f32[1,1,4,16384]{3,2,0,1:T(4,128)S(1)}, f32[1,1,4,16384]{3,2,0,1:T(4,128)S(1)}, u32[]{:S(2)}, u32[]{:S(2)}) collective-permute-start(f32[1,1,4,16384]{3,2,0,1:T(4,128)S(1)} %get-tuple-element.8), channel_id=1, source_target_pairs={{0,1},{1,2},{2,3},{3,4},{4,5},{5,6},{6,7},{7,8},{8,9},{9,10},{10,1... | collective-permute-start | bytes 786440 | tf_op jit(solution)/shard_map/ppermute | solution.py:22
  471.0 10.1 %collective-permute-start.7 = (f32[1,1,4,16384]{3,2,0,1:T(4,128)S(1)}, f32[1,1,4,16384]{3,2,0,1:T(4,128)S(1)}, u32[]{:S(2)}, u32[]{:S(2)}) collective-permute-start(f32[1,1,4,16384]{3,2,0,1:T(4,128)S(1)} %get-tuple-element.7), channel_id=1, source_target_pairs={{1,0},{2,1},{3,2},{4,3},{5,4},{6,5},{7,6},{8,7},{9,8},{10,9},{11,1... | collective-permute-start | bytes 786440 | tf_op jit(solution)/shard_map/ppermute | solution.py:24
Sparse Core Ops, SparseCore 0:
  12.7 211.5 reduce-scatter.1
